TPU v7x, 256 devices: a whole 4x4x8 slice. The times are simulated.
256 devices in a mesh: section: 4 (over z_lo, core), ctx: 64 (over y, x, z_hi).
Axes of the slice: x: 4, y: 4, z: 8 (z_hi: 4, z_lo: 2; z = z_hi * 2 + z_lo), core: 2. Of those that a mesh axis runs over, the one named last changes fastest.
Arguments:
- features: bfloat16 [4, 8192, 3, 1024], P('section', 'ctx'), may hold values from -6 to 6
- saved_conv: bfloat16 [4, 8192, 1024], P('section', 'ctx'), may hold values from -6 to 6
- grads_sent: bfloat16 [4, 8192, 1024], P('section', 'ctx'), may hold values from -6 to 6
- long_filter: float32 [4, 8192, 1024], P('section', 'ctx'), may hold values from -0.0625 to 0.0625
- short_taps: float32 [4, 3, 3, 1024], P('section'), may hold values from -3.5 to 3.5
Outputs:
- feature_grad: bfloat16 [4, 8192, 3, 1024], P('section', 'ctx')
- filter_grad: float32 [4, 8192, 1024], P('section', 'ctx')
All inputs are finite; a program needn't handle non-finite values.
Results may differ from a plain program's by a relative error of at most 0.0049.
Values may be sent and summed in bfloat16 or wider, within the bound.
No kernel may reach another device: no remote copies, remote signals or barrier semaphores. Data moves between devices by JAX's collectives and lax.ppermute only.
A program may use at most 64 MiB of HBM per device.

v0:
```python
import functools
import math

import jax
import jax.numpy as jnp
import numpy as np
from jax import lax
from jax.experimental import pallas as pl
from jax.experimental.pallas import tpu as pltpu
from jax.sharding import PartitionSpec as P

F32 = jnp.float32
BF16 = jnp.bfloat16
VMEM = pl.BlockSpec(memory_space=pltpu.VMEM)
LANES = 128


def params():
    return pltpu.CompilerParams(vmem_limit_bytes=24 * 1024 * 1024)


def two_parts(table):
    high = table.astype(np.float32).astype(BF16)
    low = (table - high.astype(np.float64)).astype(np.float32).astype(BF16)
    return high, low


def tables(blocks, rows):
    length = blocks * rows
    k1 = np.arange(blocks)
    a = np.arange(blocks)
    b = np.arange(rows)
    outer = 2 * np.pi * np.outer(k1 + 0.25, a) / blocks
    phase = 2 * np.pi * np.outer(k1 + 0.25, b) / length
    inner = 2 * np.pi * (np.outer(b, b) % rows) / rows
    cos, sin = np.cos(inner), np.sin(inner)
    first = np.concatenate([np.cos(outer), -np.sin(outer)], axis=0)
    first_high, first_low = two_parts(first)
    first_table = np.concatenate([first_high, first_low], axis=1)
    second = np.block([[cos, -sin], [sin, cos]])
    back = np.block([[cos, sin], [-sin, cos]])
    last = np.concatenate([np.cos(outer).T, -np.sin(outer).T], axis=1) / length
    phases = np.stack([np.cos(phase), np.sin(phase)]).astype(np.float32)
    return (
        first_table,
        np.stack(two_parts(second)),
        np.stack(two_parts(back)),
        np.stack(two_parts(last)),
        phases,
    )


def dot(left, right):
    return jnp.dot(left, right, preferred_element_type=F32)


def split_value(value):
    high = value.astype(BF16)
    low = (value - high.astype(F32)).astype(BF16)
    return high, low


def mixed_branch(x_ref, before_ref, taps_ref, branch, lanes):
    now = x_ref[branch, :, lanes].astype(F32)
    before = before_ref[branch, :, lanes].astype(F32)
    count = now.shape[0]
    whole = jnp.concatenate([before, now], axis=0)
    edge = before.shape[0]
    total = taps_ref[branch, 0, :, lanes] * now
    for offset in (1, 2):
        total = total + taps_ref[branch, offset, :, lanes] * whole[edge - offset : edge - offset + count]
    return total


def before_kernel(x_ref, before_ref, taps_ref, incoming_ref, filter_ref, send_ref, key_ref, value_ref):
    peers = send_ref.shape[0]
    own = send_ref.shape[1] // 3
    width = x_ref.shape[2]
    per = LANES // own
    for group in range(width // LANES):
        lanes = slice(group * LANES, (group + 1) * LANES)
        query = mixed_branch(x_ref, before_ref, taps_ref, 0, lanes)
        key = mixed_branch(x_ref, before_ref, taps_ref, 1, lanes)
        value = mixed_branch(x_ref, before_ref, taps_ref, 2, lanes)
        key_ref[:, lanes] = key
        value_ref[:, lanes] = value
        pulled = query * incoming_ref[:, lanes].astype(F32)
        for member, signal in enumerate((filter_ref[:, lanes], key * value, pulled)):
            turned = signal.T.astype(BF16).reshape(per, own, signal.shape[0])
            send_ref[group * per : (group + 1) * per, member * own : (member + 1) * own, :] = turned


def channel_kernel(own, batch, got_ref, first_ref, second_ref, back_ref, last_ref, phase_ref, out_ref, wide, result):
    blocks = phase_ref.shape[1]
    rows = phase_ref.shape[2]
    wide[...] = got_ref[...].astype(F32)
    cos = phase_ref[0]
    sin = phase_ref[1]
    first = first_ref[...]
    second_high, second_low = second_ref[0], second_ref[1]
    back_high, back_low = back_ref[0], back_ref[1]
    last_high, last_low = last_ref[0], last_ref[1]
    for start in range(0, own, batch):
        signals = [
            wide[pl.ds(member * own + start + c, blocks, stride=3 * own), :].astype(BF16)
            for member in range(3)
            for c in range(batch)
        ]
        grid = jnp.concatenate(signals, axis=1)
        outer = dot(first, jnp.concatenate([grid, grid], axis=0))
        turned = []
        for index in range(3 * batch):
            real = outer[:blocks, index * rows : (index + 1) * rows]
            imag = outer[blocks:, index * rows : (index + 1) * rows]
            turned.append(jnp.concatenate([real * cos + imag * sin, imag * cos - real * sin], axis=1))
        high, low = split_value(jnp.concatenate(turned, axis=0))
        spec = dot(high, second_high) + (dot(low, second_high) + dot(high, second_low))
        size = batch * blocks
        filter_real, filter_imag = spec[:size, :rows], spec[:size, rows:]
        product_real, product_imag = spec[size : 2 * size, :rows], spec[size : 2 * size, rows:]
        pulled_real, pulled_imag = spec[2 * size :, :rows], spec[2 * size :, rows:]
        conv = jnp.concatenate(
            [
                filter_real * pulled_real + filter_imag * pulled_imag,
                filter_real * pulled_imag - filter_imag * pulled_real,
            ],
            axis=1,
        )
        lag = jnp.concatenate(
            [
                product_real * pulled_real + product_imag * pulled_imag,
                product_real * pulled_imag - product_imag * pulled_real,
            ],
            axis=1,
        )
        high, low = split_value(jnp.concatenate([conv, lag], axis=0))
        inner = dot(high, back_high) + (dot(low, back_high) + dot(high, back_low))
        columns = []
        for index in range(2 * batch):
            real = inner[index * blocks : (index + 1) * blocks, :rows]
            imag = inner[index * blocks : (index + 1) * blocks, rows:]
            columns.append(jnp.concatenate([real * cos - imag * sin, real * sin + imag * cos], axis=0))
        high, low = split_value(jnp.concatenate(columns, axis=1))
        signal = dot(last_high, high) + (dot(last_high, low) + dot(last_low, high))
        for member in range(2):
            for c in range(batch):
                index = member * batch + c
                result[pl.ds(member * own + start + c, blocks, stride=2 * own), :] = signal[
                    :, index * rows : (index + 1) * rows
                ]
    out_ref[...] = result[...].astype(BF16)


def gathered(got_ref, group, member):
    own = got_ref.shape[1] // 2
    per = LANES // own
    piece = got_ref[group * per : (group + 1) * per, member * own : (member + 1) * own, :]
    return piece.reshape(per * own, piece.shape[2]).astype(F32).T


def branch_kernel(got_ref, key_ref, value_ref, incoming_ref, saved_ref, out_ref):
    for group in range(key_ref.shape[1] // LANES):
        lanes = slice(group * LANES, (group + 1) * LANES)
        conv = gathered(got_ref, group, 0)
        query_grad = incoming_ref[:, lanes].astype(F32) * saved_ref[:, lanes].astype(F32)
        out_ref[0, :, lanes] = query_grad.astype(BF16)
        out_ref[1, :, lanes] = (conv * value_ref[:, lanes]).astype(BF16)
        out_ref[2, :, lanes] = (conv * key_ref[:, lanes]).astype(BF16)


def lag_kernel(scale, got_ref, out_ref):
    for group in range(out_ref.shape[1] // LANES):
        lanes = slice(group * LANES, (group + 1) * LANES)
        out_ref[:, lanes] = gathered(got_ref, group, 1) * scale


def after_kernel(grads_ref, after_ref, taps_ref, out_ref):
    count = grads_ref.shape[1]
    for group in range(grads_ref.shape[2] // LANES):
        lanes = slice(group * LANES, (group + 1) * LANES)
        for branch in range(3):
            now = grads_ref[branch, :, lanes].astype(F32)
            after = after_ref[branch, :, lanes].astype(F32)
            whole = jnp.concatenate([now, after], axis=0)
            total = taps_ref[branch, 0, :, lanes] * now
            for offset in (1, 2):
                total = total + taps_ref[branch, offset, :, lanes] * whole[offset : offset + count]
            out_ref[branch, :, lanes] = total.astype(BF16)


def shape(dims, kind):
    return jax.ShapeDtypeStruct(dims, kind)


def cost(flops, moved):
    return pl.CostEstimate(flops=flops, bytes_accessed=moved, transcendentals=0)


EDGE = 8


def shards(features, saved_conv, grads_sent, long_filter, short_taps):
    sections = lax.axis_size("section")
    devices = lax.axis_size("ctx")
    incoming = lax.ppermute(grads_sent[0], "section", [(i, (i - 1) % sections) for i in range(sections)])
    local = jnp.swapaxes(features[0], 0, 1)
    _, rows, width = local.shape
    own = width // devices
    taps = short_taps[0][:, :, None, :]
    before = lax.ppermute(local[:, rows - EDGE :], "ctx", [(i, i + 1) for i in range(devices - 1)])
    send, key, value = pl.pallas_call(
        before_kernel,
        out_shape=(
            shape((devices, 3 * own, rows), BF16),
            shape((rows, width), F32),
            shape((rows, width), F32),
        ),
        in_specs=[VMEM] * 5,
        out_specs=(VMEM,) * 3,
        compiler_params=params(),
        cost_estimate=cost(20 * rows * width, 12 * rows * width),
        name="before",
    )(local, before, taps, incoming, long_filter[0])
    got = lax.all_to_all(send, "ctx", split_axis=0, concat_axis=0, tiled=True)
    constants = tables(devices, rows)
    back = pl.pallas_call(
        functools.partial(channel_kernel, own, 4),
        out_shape=shape((devices * 2 * own, rows), BF16),
        in_specs=[VMEM] * 6,
        out_specs=VMEM,
        scratch_shapes=[
            pltpu.VMEM((devices * 3 * own, rows), F32),
            pltpu.VMEM((devices * 2 * own, rows), F32),
        ],
        compiler_params=params(),
        cost_estimate=cost(4000 * rows * width, 6 * rows * width),
        name="channels",
    )(got.reshape(devices * 3 * own, rows), *constants)
    returned = lax.all_to_all(
        back.reshape(devices, 2 * own, rows), "ctx", split_axis=0, concat_axis=0, tiled=True
    )
    grads = pl.pallas_call(
        branch_kernel,
        out_shape=shape((3, rows, width), BF16),
        in_specs=[VMEM] * 5,
        out_specs=VMEM,
        compiler_params=params(),
        cost_estimate=cost(6 * rows * width, 18 * rows * width),
        name="branches",
    )(returned, key, value, incoming, saved_conv[0])
    after = lax.ppermute(grads[:, :EDGE], "ctx", [(i + 1, i) for i in range(devices - 1)])
    filter_grad = pl.pallas_call(
        functools.partial(lag_kernel, (rows * devices) ** -0.5),
        out_shape=shape((rows, width), F32),
        in_specs=[VMEM],
        out_specs=VMEM,
        compiler_params=params(),
        cost_estimate=cost(2 * rows * width, 6 * rows * width),
        name="lags",
    )(returned)
    feature_grad = pl.pallas_call(
        after_kernel,
        out_shape=shape((3, rows, width), BF16),
        in_specs=[VMEM] * 3,
        out_specs=VMEM,
        compiler_params=params(),
        cost_estimate=cost(15 * rows * width, 12 * rows * width),
        name="after",
    )(grads, after, taps)
    return (jnp.swapaxes(feature_grad, 0, 1)[None], filter_grad[None])


def solution(mesh):
    placed = (
        P("section", "ctx", None, None),
        P("section", "ctx", None),
        P("section", "ctx", None),
        P("section", "ctx", None),
        P("section", None, None, None),
    )
    return jax.shard_map(
        shards,
        mesh=mesh,
        in_specs=placed,
        out_specs=(P("section", "ctx", None, None), P("section", "ctx", None)),
        check_vma=False,
    )
```

profile of v0, /device:TPU:64, one launch (start us, length us, event | category | flops | bytes accessed | tf_op | source)
XLA Modules:
  0.0 90.9 jit_solution(15424547667640739442)
XLA Ops:
  0.6 1.4 %collective-permute-start.1 = (bf16[128,1024]{1,0:T(8,128)(2,1)}, bf16[128,1024]{1,0:T(8,128)(2,1)S(1)}, u32[]{:S(2)}, u32[]{:S(2)}) collective-permute-start(bf16[128,1024]{1,0:T(8,128)(2,1)} %bitcast.23), channel_id=1, source_target_pairs={{0,192},{64,0},{128,64},{192,128},{1,193},{65,1},{129,65},{193,129... | collective-permute-start | bytes 786440 | tf_op jit(solution)/shard_map/ppermute | solution.py:205
  2.1 0.8 slice.8
  2.9 5.5 %collective-permute-start = (bf16[3,8,1024]{2,1,0:T(8,128)(2,1)S(1)}, bf16[3,8,1024]{2,1,0:T(8,128)(2,1)S(1)}, u32[]{:S(2)}, u32[]{:S(2)}) collective-permute-start(bf16[3,8,1024]{2,1,0:T(8,128)(2,1)S(1)} %slice.8), channel_id=1, source_target_pairs={{0,1},{1,2},{2,3},{3,4},{4,5},{5,6},{6,7},{7,8},{8,9},{9,10},{10,1... | collective-permute-start | bytes 147464 | tf_op jit(solution)/shard_map/ppermute | solution.py:210
  8.4 1.7 %collective-permute-done.before_ref = bf16[3,8,1024]{2,1,0:T(8,128)(2,1)S(1)} collective-permute-done((bf16[3,8,1024]{2,1,0:T(8,128)(2,1)S(1)}, bf16[3,8,1024]{2,1,0:T(8,128)(2,1)S(1)}, u32[]{:S(2)}, u32[]{:S(2)}) %collective-permute-start) | collective-permute-done | bytes 49184 | tf_op jit(solution)/shard_map/ppermute | solution.py:210
  10.1 0.0 collective-permute-done.1.incoming_ref
  10.1 1.1 %copy-done = bf16[1,128,3,1024]{3,1,2,0:T(8,128)(2,1)S(1)} copy-done((bf16[1,128,3,1024]{3,1,2,0:T(8,128)(2,1)S(1)}, bf16[1,128,3,1024]{3,1,2,0:T(8,128)(2,1)}, u32[]{:S(2)}) %copy-start) | copy-done | bytes 786456
  11.2 1.0 %copy-done.1 = f32[1,128,1024]{2,1,0:T(8,128)S(1)} copy-done((f32[1,128,1024]{2,1,0:T(8,128)S(1)}, f32[1,128,1024]{2,1,0:T(8,128)}, u32[]{:S(2)}) %copy-start.1) | copy-done | bytes 524312
  12.3 0.7 before.1
  13.0 0.0 copy-start.2
  13.0 0.0 copy-start.3
  13.0 0.0 copy-start.6
  13.0 0.0 copy-start.7
  13.1 0.0 copy-start.8
  13.1 37.9 %all_to_all.10 = bf16[64,48,128]{2,1,0:T(8,128)(2,1)S(1)} all-to-all(bf16[64,48,128]{2,1,0:T(8,128)(2,1)S(1)} %get-tuple-element.5), channel_id=1, replica_groups=mesh['section'=4,'ctx'=64] {'ctx'}, dimensions={0} | all-to-all | bytes 1572864 | tf_op jit(solution)/shard_map/all_to_all | solution.py:224
  50.9 0.0 copy-done.6
  51.0 0.0 copy-done.7
  51.0 6.8 %channels.1 = bf16[2048,128]{1,0:T(8,128)(2,1)S(1)} custom-call(bf16[3072,128]{1,0:T(8,128)(2,1)S(1)} %bitcast.13, bf16[128,128]{1,0:T(8,128)(2,1)S(1)} %copy-done.8, bf16[2,256,256]{2,1,0:T(8,128)(2,1)S(1)} %copy-done.3, bf16[2,256,256]{2,1,0:T(8,128)(2,1)S(1)} %copy-done.2, bf16[2,64,128]{2,1,0:T(8,128)(2,1)S(1)} %copy-done.7, f32[2,64,128]{2,1,0:T(8,128)S(1)} %copy-done.6), custom_call_target="tpu_custom_call" | custom-call | flops 524288000 | bytes 786432 | tf_op jit(solution)/shard_map/channels/pallas_call | solution.py:226
  57.8 0.0 copy-start.4
  57.8 23.3 %all_to_all.11.got_ref = bf16[64,32,128]{2,1,0:T(8,128)(2,1)S(1)} all-to-all(bf16[64,32,128]{2,1,0:T(8,128)(2,1)S(1)} %bitcast.14), channel_id=1, replica_groups=mesh['section'=4,'ctx'=64] {'ctx'}, dimensions={0} | all-to-all | bytes 1048576 | tf_op jit(solution)/shard_map/all_to_all | solution.py:239
  81.0 0.3 branches.1.grads_ref
  81.3 3.6 %collective-permute-start.2 = (bf16[3,8,1024]{2,1,0:T(8,128)(2,1)S(1)}, bf16[3,8,1024]{2,1,0:T(8,128)(2,1)S(1)}, u32[]{:S(2)}, u32[]{:S(2)}) collective-permute-start(bf16[3,8,1024]{2,1,0:T(8,128)(2,1)S(1)} %slice.9), channel_id=1, source_target_pairs={{1,0},{2,1},{3,2},{4,3},{5,4},{6,5},{7,6},{8,7},{9,8},{10,9},{11,1... | collective-permute-start | bytes 147464 | tf_op jit(solution)/shard_map/ppermute | solution.py:251
  85.0 0.9 %lags.1 = f32[128,1024]{1,0:T(8,128)} custom-call(bf16[64,32,128]{2,1,0:T(8,128)(2,1)S(1)} %all_to_all.11.got_ref), custom_call_target="tpu_custom_call" | custom-call | flops 262144 | bytes 786432 | tf_op jit(solution)/shard_map/lags/pallas_call | solution.py:252
  85.9 3.5 %collective-permute-done.2.after_ref = bf16[3,8,1024]{2,1,0:T(8,128)(2,1)S(1)} collective-permute-done((bf16[3,8,1024]{2,1,0:T(8,128)(2,1)S(1)}, bf16[3,8,1024]{2,1,0:T(8,128)(2,1)S(1)}, u32[]{:S(2)}, u32[]{:S(2)}) %collective-permute-start.2) | collective-permute-done | bytes 49184 | tf_op jit(solution)/shard_map/ppermute | solution.py:251
  89.5 1.5 %after.1 = bf16[3,128,1024]{2,1,0:T(8,128)(2,1)} custom-call(bf16[3,128,1024]{2,1,0:T(8,128)(2,1)S(1)} %branches.1.grads_ref, bf16[3,8,1024]{2,1,0:T(8,128)(2,1)S(1)} %collective-permute-done.2.after_ref, f32[3,3,1,1024]{3,2,1,0:T(1,128)S(1)} %bitcast.20), custom_call_target="tpu_custom_call" | custom-call | flops 1966080 | bytes 1572864 | tf_op jit(solution)/shard_map/after/pallas_call | solution.py:261
  (9 shorter events, 0.0 us)
Async XLA Ops:
  0.6 9.5 %collective-permute-start.1 = (bf16[128,1024]{1,0:T(8,128)(2,1)}, bf16[128,1024]{1,0:T(8,128)(2,1)S(1)}, u32[]{:S(2)}, u32[]{:S(2)}) collective-permute-start(bf16[128,1024]{1,0:T(8,128)(2,1)} %bitcast.23), channel_id=1, source_target_pairs={{0,192},{64,0},{128,64},{192,128},{1,193},{65,1},{129,65},{193,129... | collective-permute-start | bytes 786440 | tf_op jit(solution)/shard_map/ppermute | solution.py:205
  2.1 8.0 %copy-start.5 = (f32[1,3,3,1024]{3,0,2,1:T(1,128)S(1)}, f32[1,3,3,1024]{3,0,2,1:T(1,128)}, u32[]{:S(2)}) copy-start(f32[1,3,3,1024]{3,0,2,1:T(1,128)} %param.14) | copy-start | bytes 110596
  2.9 7.2 %collective-permute-start = (bf16[3,8,1024]{2,1,0:T(8,128)(2,1)S(1)}, bf16[3,8,1024]{2,1,0:T(8,128)(2,1)S(1)}, u32[]{:S(2)}, u32[]{:S(2)}) collective-permute-start(bf16[3,8,1024]{2,1,0:T(8,128)(2,1)S(1)} %slice.8), channel_id=1, source_target_pairs={{0,1},{1,2},{2,3},{3,4},{4,5},{5,6},{6,7},{7,8},{8,9},{9,10},{10,1... | collective-permute-start | bytes 147464 | tf_op jit(solution)/shard_map/ppermute | solution.py:210
  10.1 1.1 %copy-start = (bf16[1,128,3,1024]{3,1,2,0:T(8,128)(2,1)S(1)}, bf16[1,128,3,1024]{3,1,2,0:T(8,128)(2,1)}, u32[]{:S(2)}) copy-start(bf16[1,128,3,1024]{3,1,2,0:T(8,128)(2,1)} %param.10) | copy-start | bytes 2359300
  11.2 1.0 %copy-start.1 = (f32[1,128,1024]{2,1,0:T(8,128)S(1)}, f32[1,128,1024]{2,1,0:T(8,128)}, u32[]{:S(2)}) copy-start(f32[1,128,1024]{2,1,0:T(8,128)} %param.13) | copy-start | bytes 1572868
  13.0 37.9 %copy-start.2 = (bf16[2,256,256]{2,1,0:T(8,128)(2,1)S(1)}, bf16[2,256,256]{2,1,0:T(8,128)(2,1)}, u32[]{:S(2)}) copy-start(bf16[2,256,256]{2,1,0:T(8,128)(2,1)} %constant.12.clone.back_ref) | copy-start | bytes 786436
  13.0 37.9 %copy-start.3 = (bf16[2,256,256]{2,1,0:T(8,128)(2,1)S(1)}, bf16[2,256,256]{2,1,0:T(8,128)(2,1)}, u32[]{:S(2)}) copy-start(bf16[2,256,256]{2,1,0:T(8,128)(2,1)} %constant.11.clone.second_ref) | copy-start | bytes 786436
  13.0 37.9 %copy-start.6 = (f32[2,64,128]{2,1,0:T(8,128)S(1)}, f32[2,64,128]{2,1,0:T(8,128)}, u32[]{:S(2)}) copy-start(f32[2,64,128]{2,1,0:T(8,128)} %constant.14.clone.phase_ref) | copy-start | bytes 196612
  13.0 37.9 %copy-start.7 = (bf16[2,64,128]{2,1,0:T(8,128)(2,1)S(1)}, bf16[2,64,128]{2,1,0:T(8,128)(2,1)}, u32[]{:S(2)}) copy-start(bf16[2,64,128]{2,1,0:T(8,128)(2,1)} %constant.13.clone.last_ref) | copy-start | bytes 98308
  13.1 37.9 %copy-start.8 = (bf16[128,128]{1,0:T(8,128)(2,1)S(1)}, bf16[128,128]{1,0:T(8,128)(2,1)}, u32[]{:S(2)}) copy-start(bf16[128,128]{1,0:T(8,128)(2,1)} %constant.10.clone.first_ref) | copy-start | bytes 98308
  57.8 23.3 %copy-start.4 = (bf16[1,128,1024]{2,1,0:T(8,128)(2,1)S(1)}, bf16[1,128,1024]{2,1,0:T(8,128)(2,1)}, u32[]{:S(2)}) copy-start(bf16[1,128,1024]{2,1,0:T(8,128)(2,1)} %param.11) | copy-start | bytes 786436
  81.3 8.1 %collective-permute-start.2 = (bf16[3,8,1024]{2,1,0:T(8,128)(2,1)S(1)}, bf16[3,8,1024]{2,1,0:T(8,128)(2,1)S(1)}, u32[]{:S(2)}, u32[]{:S(2)}) collective-permute-start(bf16[3,8,1024]{2,1,0:T(8,128)(2,1)S(1)} %slice.9), channel_id=1, source_target_pairs={{1,0},{2,1},{3,2},{4,3},{5,4},{6,5},{7,6},{8,7},{9,8},{10,9},{11,1... | collective-permute-start | bytes 147464 | tf_op jit(solution)/shard_map/ppermute | solution.py:251
where the time goes:
time: 91.3 us; the launch traced here: 90.9 us
  blocking collectives  61.1 us (67%)
  starting transfers between devices  10.6 us (12%)
  Pallas kernels  10.2 us (11%)
  waiting for transfers between devices  5.28 us (6%)
  local copies, waits for them, and re-layouts  3.03 us (3%)
    all_to_all x1, blocking collectives, shards(): got = lax.all_to_all(send, 'ctx', split_axis=0, concat_axis=0, tiled=True)  37.9 us
    all_to_all x1, blocking collectives, shards(): lax.all_to_all(back.reshape(devices, 2 * own, rows), 'ctx', split_axis=0,...  23.3 us
    pallas_call x1, Pallas kernels, shards(): pl.pallas_call(functools.partial(channel_kernel, own, 4), out_shape=shape...  6.78 us
    ppermute x1, starting transfers between devices, shards(): lax.ppermute(local[:, rows - EDGE:], 'ctx', [(i, i + 1) for i in range(de...  5.48 us
    ppermute x1, starting transfers between devices, shards(): lax.ppermute(grads[:, :EDGE], 'ctx', [(i + 1, i) for i in range(devices -...  3.64 us
    ppermute x1, waiting for transfers between devices, shards(): lax.ppermute(grads[:, :EDGE], 'ctx', [(i + 1, i) for i in range(devices -...  3.55 us
    unnamed x18, local copies, waits for them, and re-layouts  2.22 us
  transfers between devices with their start and end apart: 3, of which 2 were waited for; matrix products, arithmetic and copies ran while one was open for 1% of the time, Pallas kernels for 1%

commit v1 on v0

v1 whole, which is shorter than its diff:
```python
import functools

import jax
import jax.numpy as jnp
import numpy as np
from jax import lax
from jax.experimental import pallas as pl
from jax.experimental.pallas import tpu as pltpu
from jax.sharding import PartitionSpec as P


F32 = jnp.float32
BF16 = jnp.bfloat16
VMEM = pl.BlockSpec(memory_space=pltpu.VMEM)
LANES = 128
EDGE = 8
COLUMNS = 256


def params(size=24 * 1024):
    return pltpu.CompilerParams(vmem_limit_bytes=size * 1024)


def two_parts(table):
    high = table.astype(np.float32).astype(BF16)
    low = (table - high.astype(np.float64)).astype(np.float32).astype(BF16)
    return high, low


def stacked_parts(table, axis, order):
    parts = two_parts(table)
    return np.concatenate([parts[index] for index in order], axis=axis)


def tables(blocks, rows):
    length = blocks * rows
    k1 = np.arange(blocks)
    a = np.arange(blocks)
    b = np.arange(rows)
    outer = 2 * np.pi * np.outer(k1 + 0.25, a) / blocks
    phase = 2 * np.pi * np.outer(k1 + 0.25, b) / length
    inner = 2 * np.pi * (np.outer(b, b) % rows) / rows
    cos, sin = np.cos(inner), np.sin(inner)
    first = np.concatenate([np.cos(outer), -np.sin(outer)], axis=0)
    first_high, first_low = two_parts(first)
    first_table = np.concatenate([first_high, first_low], axis=1)
    second = np.block([[cos, -sin], [sin, cos]])
    back = np.block([[cos, sin], [-sin, cos]])
    last = np.concatenate([np.cos(outer).T, -np.sin(outer).T], axis=1) / length
    following = np.concatenate([last[1:], np.zeros_like(last[:1])], axis=0)
    phases = np.stack([np.cos(phase), np.sin(phase)]).astype(np.float32)
    return (
        first_table,
        stacked_parts(second, 0, (0, 1)),
        stacked_parts(back, 0, (0, 1)),
        np.stack([stacked_parts(each, 1, (0, 0, 1)) for each in (last, following)]),
        phases,
    )


def dot(left, right):
    return jnp.dot(left, right, preferred_element_type=F32)


def split_value(value):
    high = value.astype(BF16)
    low = (value - high.astype(F32)).astype(BF16)
    return high, low


def mixed_branch(x_ref, before_ref, taps_ref, branch, lanes):
    now = x_ref[branch, :, lanes].astype(F32)
    before = before_ref[branch, :, lanes].astype(F32)
    count = now.shape[0]
    whole = jnp.concatenate([before, now], axis=0)
    edge = before.shape[0]
    total = taps_ref[branch, 0, :, lanes] * now
    for offset in (1, 2):
        total = total + taps_ref[branch, offset, :, lanes] * whole[edge - offset : edge - offset + count]
    return total


def turned(signal, own):
    return signal.T.astype(BF16).reshape(LANES // own, own, signal.shape[0])


def fetch_kernel(x_hbm, x_ref, sem):
    copy = pltpu.make_async_copy(x_hbm, x_ref, sem)
    copy.start()
    copy.wait()


def before_kernel(
    x_ref, before_ref, taps_ref, filter_ref, incoming_ref, send_ref, key_ref, value_ref
):
    own = send_ref.shape[1] // 3
    per = LANES // own
    for group in range(x_ref.shape[2] // LANES):
        lanes = slice(group * LANES, (group + 1) * LANES)
        peers = slice(group * per, (group + 1) * per)
        query = mixed_branch(x_ref, before_ref, taps_ref, 0, lanes)
        key = mixed_branch(x_ref, before_ref, taps_ref, 1, lanes)
        value = mixed_branch(x_ref, before_ref, taps_ref, 2, lanes)
        key_ref[:, lanes] = key
        value_ref[:, lanes] = value
        upstream = incoming_ref[:, lanes].astype(F32)
        for member, signal in enumerate((filter_ref[:, lanes], key * value, query * upstream)):
            send_ref[peers, member * own : (member + 1) * own, :] = turned(signal, own)


def channel_kernel(
    own, batch, got_ref, first_ref, second_ref, back_ref, last_ref, phase_ref, out_ref, wide, result, edges
):
    blocks = phase_ref.shape[1]
    rows = phase_ref.shape[2]
    wide[...] = got_ref[...].astype(F32)
    cos = phase_ref[0]
    sin = phase_ref[1]
    first = first_ref[...]
    second = second_ref[...]
    back = back_ref[...]
    lane = lax.broadcasted_iota(jnp.int32, (2 * blocks, LANES), 1) - own * lax.rem(lax.axis_index("ctx"), LANES // own)
    ahead = [jnp.zeros((2 * blocks, LANES), F32)] * 2
    for start in range(0, own, batch):
        signals = [
            wide[pl.ds(member * own + start + c, blocks, stride=3 * own), :].astype(BF16)
            for member in range(3)
            for c in range(batch)
        ]
        grid = jnp.concatenate(signals, axis=1)
        outer = dot(first, jnp.concatenate([grid, grid], axis=0))
        pieces = []
        for index in range(3 * batch):
            real = outer[:blocks, index * rows : (index + 1) * rows]
            imag = outer[blocks:, index * rows : (index + 1) * rows]
            pieces.append(jnp.concatenate([real * cos + imag * sin, imag * cos - real * sin], axis=1))
        high = jnp.concatenate(pieces, axis=0).astype(BF16)
        spec = dot(jnp.concatenate([high, high], axis=1), second)
        size = batch * blocks
        filter_real, filter_imag = spec[:size, :rows], spec[:size, rows:]
        product_real, product_imag = spec[size : 2 * size, :rows], spec[size : 2 * size, rows:]
        pulled_real, pulled_imag = spec[2 * size :, :rows], spec[2 * size :, rows:]
        conv = jnp.concatenate(
            [
                filter_real * pulled_real + filter_imag * pulled_imag,
                filter_real * pulled_imag - filter_imag * pulled_real,
            ],
            axis=1,
        )
        lag = jnp.concatenate(
            [
                product_real * pulled_real + product_imag * pulled_imag,
                product_real * pulled_imag - product_imag * pulled_real,
            ],
            axis=1,
        )
        high = jnp.concatenate([conv, lag], axis=0).astype(BF16)
        inner = dot(jnp.concatenate([high, high], axis=1), back)
        columns = []
        for index in range(2 * batch):
            real = inner[index * blocks : (index + 1) * blocks, :rows]
            imag = inner[index * blocks : (index + 1) * blocks, rows:]
            columns.append(jnp.concatenate([real * cos - imag * sin, real * sin + imag * cos], axis=0))
        for c in range(batch):
            for j in range(2):
                ahead[j] = jnp.where(lane == start + c, columns[c][:, j : j + 1], ahead[j])
        high, low = split_value(jnp.concatenate(columns, axis=1))
        signal = dot(last_ref[0], jnp.concatenate([high, low, high], axis=0))
        for member in range(2):
            for c in range(batch):
                index = member * batch + c
                result[pl.ds(member * own + start + c, blocks, stride=2 * own), :] = signal[
                    :, index * rows : (index + 1) * rows
                ]
    out_ref[:, :own] = result[...].astype(BF16).reshape(blocks, own, 2, rows)
    high, low = split_value(jnp.concatenate(ahead, axis=1))
    further = dot(last_ref[1], jnp.concatenate([high, low, high], axis=0))
    for j in range(2):
        edges[pl.ds(j, blocks, stride=2), :] = further[:, j * LANES : (j + 1) * LANES]
    out_ref[:, own] = edges[...].astype(BF16).reshape(blocks, 2, LANES)


def after_kernel(
    scale, got_ref, key_ref, value_ref, incoming_ref, saved_ref, edge_ref, taps_ref, out_ref, filter_ref
):
    own = got_ref.shape[1] - 1
    per = LANES // own
    rows, width = key_ref.shape
    for group in range(width // LANES):
        lanes = slice(group * LANES, (group + 1) * LANES)
        peers = slice(group * per, (group + 1) * per)
        conv = got_ref[peers, : own // 2].reshape(LANES, rows).astype(F32).T
        lag = got_ref[peers, own // 2 : own].reshape(LANES, rows).astype(F32).T
        filter_ref[:, lanes] = lag * scale
        further = jnp.sum(got_ref[peers, own].astype(F32), axis=0)
        further = jnp.concatenate([further, jnp.zeros((EDGE - 2, LANES), F32)], axis=0)
        grads = (
            incoming_ref[:, lanes].astype(F32) * saved_ref[:, lanes].astype(F32),
            conv * value_ref[:, lanes],
            conv * key_ref[:, lanes],
        )
        after = (
            edge_ref[0, :, lanes],
            further * edge_ref[2, :, lanes],
            further * edge_ref[1, :, lanes],
        )
        for branch in range(3):
            whole = jnp.concatenate([grads[branch], after[branch]], axis=0).astype(BF16).astype(F32)
            total = taps_ref[branch, 0, :, lanes] * whole[:rows]
            for offset in (1, 2):
                total = total + taps_ref[branch, offset, :, lanes] * whole[offset : offset + rows]
            out_ref[branch, :, lanes] = total.astype(BF16)


def shape(dims, kind):
    return jax.ShapeDtypeStruct(dims, kind)


def cost(flops, moved):
    return pl.CostEstimate(flops=flops, bytes_accessed=moved, transcendentals=0)


def section_part(features, saved_conv, grads_sent, long_filter, short_taps):
    sections = lax.axis_size("section")
    devices = lax.axis_size("ctx")
    incoming = lax.ppermute(grads_sent[0], "section", [(i, (i - 1) % sections) for i in range(sections)])
    local = jnp.swapaxes(features[0], 0, 1)
    _, rows, width = local.shape
    own = width // devices
    taps = short_taps[0][:, :, None, :]
    before = lax.ppermute(local[:, rows - EDGE :], "ctx", [(i, i + 1) for i in range(devices - 1)])
    outside = pl.BlockSpec(memory_space=pltpu.HBM)
    held = pl.pallas_call(
        fetch_kernel,
        out_shape=shape((3, rows, width), BF16),
        in_specs=[outside],
        out_specs=VMEM,
        scratch_shapes=[pltpu.SemaphoreType.DMA],
        compiler_params=params(54100),
        cost_estimate=cost(0, 20 * rows * width),
        name="fetch",
    )(local)
    send, key, value = pl.pallas_call(
        before_kernel,
        out_shape=(
            shape((devices, 3 * own, rows), BF16),
            shape((rows, width), F32),
            shape((rows, width), F32),
        ),
        in_specs=[VMEM] * 5,
        out_specs=(VMEM,) * 3,
        compiler_params=params(),
        cost_estimate=cost(20 * rows * width, 12 * rows * width),
        name="before",
    )(held, before, taps, long_filter[0], incoming)
    got = lax.all_to_all(send, "ctx", split_axis=0, concat_axis=0, tiled=True)
    query_edge = incoming[:EDGE].astype(F32) * saved_conv[0, :EDGE].astype(F32)
    edge = jnp.stack([query_edge, key[:EDGE], value[:EDGE]])
    edge = lax.ppermute(edge, "ctx", [(i + 1, i) for i in range(devices - 1)])
    back = pl.pallas_call(
        functools.partial(channel_kernel, own, 8),
        out_shape=shape((devices, own + 1, 2, rows), BF16),
        in_specs=[VMEM] * 6,
        out_specs=VMEM,
        scratch_shapes=[
            pltpu.VMEM((devices * 3 * own, rows), F32),
            pltpu.VMEM((devices * 2 * own, rows), F32),
            pltpu.VMEM((devices * 2, LANES), F32),
        ],
        compiler_params=params(),
        cost_estimate=cost(4000 * rows * width, 6 * rows * width),
        name="channels",
    )(got.reshape(devices * 3 * own, rows), *tables(devices, rows))
    returned = lax.all_to_all(back, "ctx", split_axis=0, concat_axis=0, tiled=True)
    steps = width // COLUMNS
    wide_block = pl.BlockSpec((rows, COLUMNS), lambda i: (0, i))
    deep_block = pl.BlockSpec((3, rows, COLUMNS), lambda i: (0, 0, i))
    feature_grad, filter_grad = pl.pallas_call(
        functools.partial(after_kernel, (rows * devices) ** -0.5),
        grid=(steps,),
        out_shape=(shape((3, rows, width), BF16), shape((rows, width), F32)),
        in_specs=[
            pl.BlockSpec((devices // steps, own + 1, 2, rows), lambda i: (i, 0, 0, 0)),
            wide_block,
            wide_block,
            wide_block,
            wide_block,
            pl.BlockSpec((3, EDGE, COLUMNS), lambda i: (0, 0, i)),
            pl.BlockSpec((3, 3, 1, COLUMNS), lambda i: (0, 0, 0, i)),
        ],
        out_specs=(deep_block, wide_block),
        compiler_params=params(),
        cost_estimate=cost(25 * rows * width, 22 * rows * width),
        name="after",
    )(returned, key, value, incoming, saved_conv[0], edge, taps)
    return (jnp.swapaxes(feature_grad, 0, 1)[None], filter_grad[None])


def solution(mesh):
    placed = (
        P("section", "ctx", None, None),
        P("section", "ctx", None),
        P("section", "ctx", None),
        P("section", "ctx", None),
        P("section", None, None, None),
    )
    return jax.shard_map(
        section_part,
        mesh=mesh,
        in_specs=placed,
        out_specs=(P("section", "ctx", None, None), P("section", "ctx", None)),
        check_vma=False,
    )
```

time: 91.3 us -> 83.8 us (0.918)
  blocking collectives: 61.1 us -> 37.9 us
  waiting for transfers between devices: 5.28 us -> 17.8 us
  starting transfers between devices: 10.6 us -> 15.7 us
  local copies, waits for them, and re-layouts: 3.03 us -> 0.85 us
    all_to_all x2 -> x1, blocking collectives: 61.1 us -> 37.9 us  [section_part(): got = lax.all_to_all(send, 'ctx', split_axis=0, concat_axis=0, tiled=True)]
    ppermute x3, waiting for transfers between devices: 5.28 us -> 15.1 us  [the longest x1 14.5 us: section_part(): edge = lax.ppermute(edge, 'ctx', [(i + 1, i) for i in range(devices - 1)])]
    all_to_all x0 -> x1, starting transfers between devices: none -> 6.29 us  [section_part(): lax.all_to_all(back, 'ctx', split_axis=0, concat_axis=0, tiled=True)]
    all_to_all x0 -> x1, waiting for transfers between devices: none -> 2.73 us  [section_part(): lax.all_to_all(back, 'ctx', split_axis=0, concat_axis=0, tiled=True)]
    unnamed x18 -> x16, local copies, waits for them, and re-layouts: 2.22 us -> 0.05 us
    ppermute x3, starting transfers between devices: 10.6 us -> 9.41 us  [the longest x1 5.61 us: section_part(): lax.ppermute(local[:, rows - EDGE:], 'ctx', [(i, i + 1) for i in range(de...]
    pallas_call x5 -> x4, Pallas kernels: 10.2 us -> 9.92 us  [the longest x1 5.64 us: section_part(): pl.pallas_call(functools.partial(channel_kernel, own, 8), out_shape=shape...]
  transfers between devices with their start and end apart: 3 -> 4, of which waited for: 2 -> 3; matrix products, arithmetic and copies ran while one was open for 1% -> 1% of each run, Pallas kernels for 1% -> 1%
where the time goes in v1:
time: 83.8 us; the launch traced here: 82.9 us
  blocking collectives  37.9 us (45%)
  waiting for transfers between devices  17.8 us (21%)
  starting transfers between devices  15.7 us (19%)
  Pallas kernels  9.92 us (12%)
  local copies, waits for them, and re-layouts  0.85 us (1%)
    all_to_all x1, blocking collectives, section_part(): got = lax.all_to_all(send, 'ctx', split_axis=0, concat_axis=0, tiled=True)  37.9 us
    ppermute x1, waiting for transfers between devices, section_part(): edge = lax.ppermute(edge, 'ctx', [(i + 1, i) for i in range(devices - 1)])  14.5 us
    all_to_all x1, starting transfers between devices, section_part(): lax.all_to_all(back, 'ctx', split_axis=0, concat_axis=0, tiled=True)  6.29 us
    pallas_call x1, Pallas kernels, section_part(): pl.pallas_call(functools.partial(channel_kernel, own, 8), out_shape=shape...  5.64 us
    ppermute x1, starting transfers between devices, section_part(): lax.ppermute(local[:, rows - EDGE:], 'ctx', [(i, i + 1) for i in range(de...  5.61 us
    all_to_all x1, waiting for transfers between devices, section_part(): lax.all_to_all(back, 'ctx', split_axis=0, concat_axis=0, tiled=True)  2.73 us
    pallas_call x1, Pallas kernels, section_part(): pl.pallas_call(functools.partial(after_kernel, (rows * devices) ** (-0.5)...  2.41 us
    ppermute x1, starting transfers between devices, section_part(): edge = lax.ppermute(edge, 'ctx', [(i + 1, i) for i in range(devices - 1)])  2.36 us
  transfers between devices with their start and end apart: 4, of which 3 were waited for; matrix products, arithmetic and copies ran while one was open for 1% of the time, Pallas kernels for 1%

profile of v1, /device:TPU:64, one launch (start us, length us, event | category | flops | bytes accessed | tf_op | source)
XLA Modules:
  0.0 82.9 jit_solution(12569278100574330879)
XLA Ops:
  0.6 1.4 %collective-permute-start.1 = (bf16[128,1024]{1,0:T(8,128)(2,1)}, bf16[128,1024]{1,0:T(8,128)(2,1)S(1)}, u32[]{:S(2)}, u32[]{:S(2)}) collective-permute-start(bf16[128,1024]{1,0:T(8,128)(2,1)} %bitcast.30), channel_id=1, source_target_pairs={{0,192},{64,0},{128,64},{192,128},{1,193},{65,1},{129,65},{193,129... | collective-permute-start | bytes 786440 | tf_op jit(solution)/shard_map/ppermute | solution.py:226
  2.1 0.8 slice.20
  2.9 5.6 %collective-permute-start = (bf16[3,8,1024]{2,1,0:T(8,128)(2,1)S(1)}, bf16[3,8,1024]{2,1,0:T(8,128)(2,1)S(1)}, u32[]{:S(2)}, u32[]{:S(2)}) collective-permute-start(bf16[3,8,1024]{2,1,0:T(8,128)(2,1)S(1)} %slice.20), channel_id=1, source_target_pairs={{0,1},{1,2},{2,3},{3,4},{4,5},{5,6},{6,7},{7,8},{8,9},{9,10},{10,1... | collective-permute-start | bytes 147464 | tf_op jit(solution)/shard_map/ppermute | solution.py:231
  8.5 1.1 %fetch.1.x_ref = bf16[3,128,1024]{2,1,0:T(8,128)(2,1)S(1)} custom-call(bf16[3,128,1024]{2,1,0:T(8,128)(2,1)} %bitcast.27), custom_call_target="tpu_custom_call" | custom-call | bytes 2621440 | tf_op jit(solution)/shard_map/fetch/pallas_call | solution.py:233
  9.6 0.6 collective-permute-done.before_ref
  10.2 0.0 collective-permute-done.1.incoming_ref
  10.2 0.0 copy-done
  10.2 0.0 copy-done.4
  10.2 0.7 before.1
  11.0 0.0 copy-start.2
  11.0 0.0 copy-start.3
  11.0 0.0 copy-start.5
  11.0 0.0 copy-start.6
  11.0 0.0 copy-start.7
  11.0 37.9 %all_to_all.10 = bf16[64,48,128]{2,1,0:T(8,128)(2,1)S(1)} all-to-all(bf16[64,48,128]{2,1,0:T(8,128)(2,1)S(1)} %get-tuple-element.7), channel_id=1, replica_groups=mesh['section'=4,'ctx'=64] {'ctx'}, dimensions={0} | all-to-all | bytes 1572864 | tf_op jit(solution)/shard_map/all_to_all | solution.py:256
  48.9 0.0 copy-done.2
  48.9 0.0 copy-done.5
  48.9 5.6 %channels.1 = bf16[64,17,2,128]{3,2,1,0:T(2,128)(2,1)} custom-call(bf16[3072,128]{1,0:T(8,128)(2,1)S(1)} %bitcast.21, bf16[128,128]{1,0:T(8,128)(2,1)S(1)} %copy-done.7, bf16[512,256]{1,0:T(8,128)(2,1)S(1)} %copy-done.3, bf16[512,256]{1,0:T(8,128)(2,1)S(1)} %copy-done.2, bf16[2,64,384]{2,1,0:T(8,128)(2,1)S(1)} %copy-done.5, f32[2,64,128]{2,1,0:T(8,128)S(1)} %copy-done.6), custom_call_target="tpu_custom_call" | custom-call | flops 524288000 | bytes 786432 | tf_op jit(solution)/shard_map/channels/pallas_call | solution.py:260
  54.6 6.3 %all-to-all-start.1 = ((bf16[64,17,2,128]{3,2,1,0:T(2,128)(2,1)}), bf16[64,17,2,128]{3,2,1,0:T(2,128)(2,1)S(1)}, u32[]{:S(2)}, u32[]{:S(2)}) async-start(bf16[64,17,2,128]{3,2,1,0:T(2,128)(2,1)} %channels.1), calls=%async_computation.1 | async-start | bytes 1114112 | tf_op jit(solution)/shard_map/all_to_all | solution.py:274
  60.9 0.0 copy-done.1
  60.9 2.4 %collective-permute-start.2 = (f32[3,8,1024]{2,1,0:T(8,128)S(1)}, f32[3,8,1024]{2,1,0:T(8,128)S(1)}, u32[]{:S(2)}, u32[]{:S(2)}) collective-permute-start(f32[3,8,1024]{2,1,0:T(8,128)S(1)} %pad_maximum_fusion), channel_id=1, source_target_pairs={{1,0},{2,1},{3,2},{4,3},{5,4},{6,5},{7,6},{8,7},{9,8},{10,9},{11,1... | collective-permute-start | bytes 294920 | tf_op jit(solution)/shard_map/ppermute | solution.py:259
  63.3 14.5 %collective-permute-done.2.edge_ref = f32[3,8,1024]{2,1,0:T(8,128)S(1)} collective-permute-done((f32[3,8,1024]{2,1,0:T(8,128)S(1)}, f32[3,8,1024]{2,1,0:T(8,128)S(1)}, u32[]{:S(2)}, u32[]{:S(2)}) %collective-permute-start.2) | collective-permute-done | bytes 98336 | tf_op jit(solution)/shard_map/ppermute | solution.py:259
  77.8 2.7 %all-to-all-done.1.got_ref = bf16[64,17,2,128]{3,2,1,0:T(2,128)(2,1)S(1)} async-done(((bf16[64,17,2,128]{3,2,1,0:T(2,128)(2,1)}), bf16[64,17,2,128]{3,2,1,0:T(2,128)(2,1)S(1)}, u32[]{:S(2)}, u32[]{:S(2)}) %all-to-all-start.1) | async-done | bytes 557088 | tf_op jit(solution)/shard_map/all_to_all | solution.py:274
  80.5 2.4 %after.1 = (bf16[3,128,1024]{2,1,0:T(8,128)(2,1)}, f32[128,1024]{1,0:T(8,128)}) custom-call(bf16[64,17,2,128]{3,2,1,0:T(2,128)(2,1)S(1)} %all-to-all-done.1.got_ref, f32[128,1024]{1,0:T(8,128)S(1)} %get-tuple-element.8.key_ref, f32[128,1024]{1,0:T(8,128)S(1)} %get-tuple-element.9.value_ref, bf16[128,1024]{1,0:T(8,128)(2,1)S(1)} %collective-permute-done.1.incoming_ref, ...), custom_call_target="tpu_custom_call" | custom-call | flops 3276800 | bytes 2883584 | tf_op jit(solution)/shard_map/after/pallas_call | solution.py:278
  (9 shorter events, 0.0 us)
Async XLA Ops:
  0.6 9.6 %collective-permute-start.1 = (bf16[128,1024]{1,0:T(8,128)(2,1)}, bf16[128,1024]{1,0:T(8,128)(2,1)S(1)}, u32[]{:S(2)}, u32[]{:S(2)}) collective-permute-start(bf16[128,1024]{1,0:T(8,128)(2,1)} %bitcast.30), channel_id=1, source_target_pairs={{0,192},{64,0},{128,64},{192,128},{1,193},{65,1},{129,65},{193,129... | collective-permute-start | bytes 786440 | tf_op jit(solution)/shard_map/ppermute | solution.py:226
  2.9 7.4 %copy-start = (f32[1,128,1024]{2,1,0:T(8,128)S(1)}, f32[1,128,1024]{2,1,0:T(8,128)}, u32[]{:S(2)}) copy-start(f32[1,128,1024]{2,1,0:T(8,128)} %param.13) | copy-start | bytes 1572868
  2.9 7.4 %copy-start.4 = (f32[1,3,3,1024]{3,0,2,1:T(1,128)S(1)}, f32[1,3,3,1024]{3,0,2,1:T(1,128)}, u32[]{:S(2)}) copy-start(f32[1,3,3,1024]{3,0,2,1:T(1,128)} %param.14) | copy-start | bytes 110596
  2.9 7.3 %collective-permute-start = (bf16[3,8,1024]{2,1,0:T(8,128)(2,1)S(1)}, bf16[3,8,1024]{2,1,0:T(8,128)(2,1)S(1)}, u32[]{:S(2)}, u32[]{:S(2)}) collective-permute-start(bf16[3,8,1024]{2,1,0:T(8,128)(2,1)S(1)} %slice.20), channel_id=1, source_target_pairs={{0,1},{1,2},{2,3},{3,4},{4,5},{5,6},{6,7},{7,8},{8,9},{9,10},{10,1... | collective-permute-start | bytes 147464 | tf_op jit(solution)/shard_map/ppermute | solution.py:231
  11.0 37.9 %copy-start.2 = (bf16[512,256]{1,0:T(8,128)(2,1)S(1)}, bf16[512,256]{1,0:T(8,128)(2,1)}, u32[]{:S(2)}) copy-start(bf16[512,256]{1,0:T(8,128)(2,1)} %constant.12.clone.back_ref) | copy-start | bytes 786436
  11.0 37.9 %copy-start.3 = (bf16[512,256]{1,0:T(8,128)(2,1)S(1)}, bf16[512,256]{1,0:T(8,128)(2,1)}, u32[]{:S(2)}) copy-start(bf16[512,256]{1,0:T(8,128)(2,1)} %constant.11.clone.second_ref) | copy-start | bytes 786436
  11.0 37.9 %copy-start.5 = (bf16[2,64,384]{2,1,0:T(8,128)(2,1)S(1)}, bf16[2,64,384]{2,1,0:T(8,128)(2,1)}, u32[]{:S(2)}) copy-start(bf16[2,64,384]{2,1,0:T(8,128)(2,1)} %constant.13.clone.last_ref) | copy-start | bytes 294916
  11.0 37.9 %copy-start.6 = (f32[2,64,128]{2,1,0:T(8,128)S(1)}, f32[2,64,128]{2,1,0:T(8,128)}, u32[]{:S(2)}) copy-start(f32[2,64,128]{2,1,0:T(8,128)} %constant.14.clone.phase_ref) | copy-start | bytes 196612
  11.0 37.9 %copy-start.7 = (bf16[128,128]{1,0:T(8,128)(2,1)S(1)}, bf16[128,128]{1,0:T(8,128)(2,1)}, u32[]{:S(2)}) copy-start(bf16[128,128]{1,0:T(8,128)(2,1)} %constant.10.clone.first_ref) | copy-start | bytes 98308
  54.6 6.3 %copy-start.1 = (bf16[1,128,1024]{2,1,0:T(8,128)(2,1)S(1)}, bf16[1,128,1024]{2,1,0:T(8,128)(2,1)}, u32[]{:S(2)}) copy-start(bf16[1,128,1024]{2,1,0:T(8,128)(2,1)} %param.11) | copy-start | bytes 786436
  54.6 25.9 %all-to-all-start.1 = ((bf16[64,17,2,128]{3,2,1,0:T(2,128)(2,1)}), bf16[64,17,2,128]{3,2,1,0:T(2,128)(2,1)S(1)}, u32[]{:S(2)}, u32[]{:S(2)}) async-start(bf16[64,17,2,128]{3,2,1,0:T(2,128)(2,1)} %channels.1), calls=%async_computation.1 | async-start | bytes 1114112 | tf_op jit(solution)/shard_map/all_to_all | solution.py:274
  60.9 16.8 %collective-permute-start.2 = (f32[3,8,1024]{2,1,0:T(8,128)S(1)}, f32[3,8,1024]{2,1,0:T(8,128)S(1)}, u32[]{:S(2)}, u32[]{:S(2)}) collective-permute-start(f32[3,8,1024]{2,1,0:T(8,128)S(1)} %pad_maximum_fusion), channel_id=1, source_target_pairs={{1,0},{2,1},{3,2},{4,3},{5,4},{6,5},{7,6},{8,7},{9,8},{10,9},{11,1... | collective-permute-start | bytes 294920 | tf_op jit(solution)/shard_map/ppermute | solution.py:259
